TPU v7x, 32 devices: a whole 2x2x4 slice. The times are simulated.
32 devices in a mesh: expert: 8 (over z, core), tensor: 4 (over y, x).
Axes of the slice: x: 2, y: 2, z: 4, core: 2. Of those that a mesh axis runs over, the one named last changes fastest.
Arguments:
- tokens: bfloat16 [256, 4096], P('expert', 'tensor'), may hold values from -6 to 6
- cotangent: bfloat16 [256, 4096], P('expert', 'tensor'), may hold values from -6 to 6
- expert_ids: int32 [256, 8], P('expert'), may hold values from 0 to 63, all different within a row; in each aligned block of 32 rows (0 to 31, 32 to 63, ...) at most 8 rows name the same one
- route_weight: float32 [256, 8], P('expert'), may hold values from 0.05 to 0.25
- w_gate: bfloat16 [64, 4096, 1536], P('expert', 'tensor'), may hold values from -0.09375 to 0.09375
- w_up: bfloat16 [64, 4096, 1536], P('expert', 'tensor'), may hold values from -0.09375 to 0.09375
- w_down: bfloat16 [64, 1536, 4096], P('expert', None, 'tensor'), may hold values from -0.15625 to 0.15625
Outputs:
- mixed_out: bfloat16 [256, 4096], P('expert', 'tensor')
- input_grad: bfloat16 [256, 4096], P('expert', 'tensor')
- down_grad: bfloat16 [64, 1536, 4096], P('expert', None, 'tensor')
Inputs may be any that keep to these rules, and one draw needn't show every extreme that they name: `expert_ids`: each row names 8 different experts; within the 32 rows of one device no expert is named more than 8 times.
All inputs are finite; a program needn't handle non-finite values.
Results may differ from a plain program's by a relative error of at most 0.023.
Values may be sent and summed in bfloat16 or wider, within the bound.
No kernel may reach another device: no remote copies, remote signals or barrier semaphores. Data moves between devices by JAX's collectives and lax.ppermute only.
A program may use at most 192 MiB of HBM per device.

v0:
```python
import jax
import jax.numpy as jnp
from jax import lax
from jax.sharding import PartitionSpec as P


def local(tokens, cotangent, expert_ids, route_weight, w_gate, w_up, w_down):
    resident_specialists = w_gate.shape[0]
    experts = resident_specialists * lax.axis_size("expert")
    tok_count = expert_ids.shape[0]
    top_count = expert_ids.shape[1]
    capacity = 2 * tok_count * top_count // experts
    model_width = tokens.shape[1]
    flat_ids = expert_ids.reshape(-1)
    onehot = (flat_ids[:, None] == jnp.arange(experts, dtype=jnp.int32)[None, :]).astype(jnp.int32)
    before = jnp.cumsum(onehot, axis=0) - onehot
    slot_index = jnp.sum(before * onehot, axis=1)
    target = flat_ids * capacity + slot_index
    chosen = (target[:, None] == jnp.arange(experts * capacity, dtype=jnp.int32)[None, :]).astype(
        jnp.float32
    )
    chosen = chosen.reshape(tok_count, top_count, experts * capacity)
    expert_assignment = jnp.sum(chosen, axis=1)
    weighted = jnp.sum(chosen * route_weight[:, :, None], axis=1)
    token_send = jnp.dot(
        expert_assignment.T.astype(jnp.bfloat16), tokens, preferred_element_type=jnp.float32
    )
    token_send = token_send.astype(jnp.bfloat16).reshape(experts, capacity, model_width)
    gradient_outgoing = jnp.dot(
        weighted.T, cotangent, precision=lax.Precision.HIGHEST, preferred_element_type=jnp.float32
    )
    gradient_outgoing = gradient_outgoing.astype(jnp.bfloat16).reshape(
        experts, capacity, model_width
    )
    token_rows, grad_rows = (
        lax.all_to_all(token_send, "expert", split_axis=0, concat_axis=1, tiled=True),
        lax.all_to_all(gradient_outgoing, "expert", split_axis=0, concat_axis=1, tiled=True),
    )
    pre_gate = jnp.einsum("erd,edf->erf", token_rows, w_gate, preferred_element_type=jnp.float32)
    pre_up = jnp.einsum("erd,edf->erf", token_rows, w_up, preferred_element_type=jnp.float32)
    slice_breadth = w_gate.shape[2] // lax.axis_size("tensor")
    gate_sum, up_sum = (
        lax.psum(pre_gate.astype(jnp.bfloat16), "tensor").astype(jnp.float32),
        lax.psum(pre_up.astype(jnp.bfloat16), "tensor").astype(jnp.float32),
    )
    sigmoid_all = jax.nn.sigmoid(gate_sum)
    hidden = (gate_sum * sigmoid_all * up_sum).astype(jnp.bfloat16)
    out_rows = jnp.einsum(
        "erf,efd->erd", hidden, w_down, preferred_element_type=jnp.float32
    ).astype(jnp.bfloat16)
    down_grad = jnp.einsum("erf,erd->efd", hidden, grad_rows, preferred_element_type=jnp.float32)
    offset = lax.axis_index("tensor") * slice_breadth
    gate_part = lax.dynamic_slice_in_dim(gate_sum, offset, slice_breadth, 2)
    up_part = lax.dynamic_slice_in_dim(up_sum, offset, slice_breadth, 2)
    sigmoid_part = lax.dynamic_slice_in_dim(sigmoid_all, offset, slice_breadth, 2)
    hidden_term = jnp.einsum("erd,efd->erf", grad_rows, w_down, preferred_element_type=jnp.float32)
    hidden_grad = lax.psum_scatter(
        hidden_term.astype(jnp.bfloat16), "tensor", scatter_dimension=2, tiled=True
    ).astype(jnp.float32)
    gate_grad = (
        hidden_grad * up_part * sigmoid_part * (1.0 + gate_part * (1.0 - sigmoid_part))
    ).astype(jnp.bfloat16)
    up_grad = (hidden_grad * gate_part * sigmoid_part).astype(jnp.bfloat16)
    gate_piece = lax.all_gather(gate_grad, "tensor", axis=2, tiled=True)
    up_piece = lax.all_gather(up_grad, "tensor", axis=2, tiled=True)
    running = jnp.einsum("erf,edf->erd", gate_piece, w_gate, preferred_element_type=jnp.float32)
    input_rows = running + jnp.einsum(
        "erf,edf->erd", up_piece, w_up, preferred_element_type=jnp.float32
    )
    input_rows = input_rows.astype(jnp.bfloat16)
    returned_out, returned_in = (
        lax.all_to_all(out_rows, "expert", split_axis=1, concat_axis=0, tiled=True),
        lax.all_to_all(input_rows, "expert", split_axis=1, concat_axis=0, tiled=True),
    )
    returned_out = returned_out.reshape(experts * capacity, model_width)
    returned_in = returned_in.reshape(experts * capacity, model_width)
    mixed_out = jnp.dot(
        weighted, returned_out, precision=lax.Precision.HIGHEST, preferred_element_type=jnp.float32
    )
    input_grad = jnp.dot(
        expert_assignment.astype(jnp.bfloat16), returned_in, preferred_element_type=jnp.float32
    )
    return (
        mixed_out.astype(jnp.bfloat16),
        input_grad.astype(jnp.bfloat16),
        down_grad.astype(jnp.bfloat16),
    )


def solution(mesh):
    return jax.shard_map(
        local,
        mesh=mesh,
        in_specs=(
            P("expert", "tensor"),
            P("expert", "tensor"),
            P("expert", None),
            P("expert", None),
            P("expert", "tensor", None),
            P("expert", "tensor", None),
            P("expert", None, "tensor"),
        ),
        out_specs=(P("expert", "tensor"), P("expert", "tensor"), P("expert", None, "tensor")),
        check_vma=False,
    )
```

profile of v0, /device:TPU:0, one launch (start us, length us, event | category | flops | bytes accessed | tf_op | source)
XLA Modules:
  0.0 326.9 jit_solution(5938493697258200641)
XLA Ops:
  7.2 0.0 copy-start
  7.2 0.0 copy-start.6
  7.2 0.8 copy.45
  8.0 0.1 eq.43
  8.1 0.1 eq.39
  8.2 0.8 copy.49
  8.9 0.6 reduce-window.6
  9.6 0.2 slice_reduce_fusion
  9.8 0.1 fusion.17
  9.9 0.1 reduce_sum.30
  10.0 0.4 convert_reduce_fusion
  10.4 0.0 copy-start.4
  10.4 0.6 copy-done.4
  11.0 0.0 copy-done
  11.0 1.4 fusion
  12.4 6.4 %all-to-all-start = ((bf16[64,8,1024]{2,1,0:T(8,128)(2,1)}), bf16[64,8,1024]{2,1,0:T(8,128)(2,1)S(1)}, u32[]{:S(2)}, u32[]{:S(2)}) async-start(bf16[64,8,1024]{2,1,0:T(8,128)(2,1)} %fusion), calls=%async_computation | async-start | bytes 2097152 | tf_op jit(solution)/shard_map/all_to_all | solution.py:36
  18.8 0.0 copy-done.6
  18.8 2.0 fusion.1
  20.8 24.5 %all-to-all-done = bf16[64,8,1024]{2,1,0:T(8,128)(2,1)S(1)} async-done(((bf16[64,8,1024]{2,1,0:T(8,128)(2,1)}), bf16[64,8,1024]{2,1,0:T(8,128)(2,1)S(1)}, u32[]{:S(2)}, u32[]{:S(2)}) %all-to-all-start) | async-done | bytes 1048608 | tf_op jit(solution)/shard_map/all_to_all | solution.py:36
  45.4 3.6 %all-to-all-start.2 = ((bf16[64,8,1024]{2,1,0:T(8,128)(2,1)}), bf16[64,8,1024]{2,1,0:T(8,128)(2,1)S(1)}, u32[]{:S(2)}, u32[]{:S(2)}) async-start(bf16[64,8,1024]{2,1,0:T(8,128)(2,1)} %fusion.1), calls=%async_computation.2 | async-start | bytes 2097152 | tf_op jit(solution)/shard_map/all_to_all | solution.py:37
  48.9 0.0 all-reduce.3.cloned.1.call-start
  49.0 13.7 %convolution_convert_fusion.2 = bf16[8,64,1536]{2,1,0:T(8,128)(2,1)} fusion(bf16[8,1024,1536]{2,1,0:T(8,128)(2,1)} %param.12, bf16[8,8,8,1024]{3,2,1,0:T(8,128)(2,1)S(1)} %bitcast.68), kind=kOutput, calls=%fused_computation.4 | convolution fusion | flops 1611399168 | bytes 27787264 | tf_op jit(solution)/shard_map/erd,edf->erf/dot_general | solution.py:40
  62.7 13.7 %convolution_convert_fusion.3 = bf16[8,64,1536]{2,1,0:T(8,128)(2,1)} fusion(bf16[8,1024,1536]{2,1,0:T(8,128)(2,1)} %param.11, bf16[8,8,8,1024]{3,2,1,0:T(8,128)(2,1)S(1)} %bitcast.69), kind=kOutput, calls=%fused_computation.5 | convolution fusion | flops 1611399168 | bytes 27787264 | tf_op jit(solution)/shard_map/erd,edf->erf/dot_general | solution.py:39
  76.4 0.0 all-reduce.3.cloned.1.call-update
  76.4 0.0 reduce-scatter.4.cloned.1.call-start
  76.5 0.0 all-to-all-done.2
  76.5 13.2 %convolution_convert_fusion.1 = bf16[8,64,1536]{2,1,0:T(8,128)(2,1)S(1)} fusion(bf16[8,1536,1024]{2,1,0:T(8,128)(2,1)} %param.13, bf16[8,8,8,1024]{3,2,1,0:T(8,128)(2,1)S(1)} %bitcast.65), kind=kOutput, calls=%fused_computation.3 | convolution fusion | flops 1611399168 | bytes 27787264 | tf_op jit(solution)/shard_map/erd,efd->erf/dot_general | solution.py:56
  89.7 3.5 %copy.60 = bf16[8,64,1536]{1,0,2:T(8,128)(2,1)} copy(bf16[8,64,1536]{2,1,0:T(8,128)(2,1)S(1)} %convolution_convert_fusion.1) | data formatting | bytes 3145728
  93.2 5.4 %reshape.61 = bf16[1536,512]{1,0:T(8,128)(2,1)} reshape(bf16[1536,8,64]{2,1,0:T(8,128)(2,1)} %bitcast.67) | data formatting | bytes 3145728
  98.6 0.0 reduce-scatter.4.cloned.1.call-update
  98.6 0.2 all-gather.3.cloned.1.call-start
  98.9 66.0 %all-reduce.3.cloned.1.call-done = (bf16[8,64,1536]{2,1,0:T(8,128)(2,1)}, bf16[8,64,1536]{2,1,0:T(8,128)(2,1)}) async-done(((bf16[8,64,1536]{2,1,0:T(8,128)(2,1)}, bf16[8,64,1536]{2,1,0:T(8,128)(2,1)}), (bf16[8,64,1536]{2,1,0:T(8,128)(2,1)}, bf16[8,64,1536]{2,1,0:T(8,128)(2,1)})) %all-reduce.3.cloned.1.call-update) | async-done | bytes 3145744 | tf_op jit(solution)/shard_map/psum | solution.py:43
  164.9 0.0 copy-start.2
  164.9 3.6 %convert_element_type.70 = f32[8,64,1536]{2,1,0:T(8,128)} convert(bf16[8,64,1536]{2,1,0:T(8,128)(2,1)} %get-tuple-element.5) | non-fusion elementwise | flops 786432 | bytes 4718592 | tf_op jit(solution)/shard_map/convert_element_type | solution.py:43
  168.5 0.0 copy-done.2
  168.5 2.5 add_divide_fusion
  171.0 28.1 %reduce-scatter.4.cloned.1.call-done = bf16[384,512]{1,0:T(8,128)(2,1)} async-done(((bf16[1536,512]{1,0:T(8,128)(2,1)}), bf16[384,512]{1,0:T(8,128)(2,1)}) %reduce-scatter.4.cloned.1.call-update) | async-done | bytes 393232
  199.0 1.5 reshape.62
  200.6 1.3 copy.61
  201.8 0.0 copy-start.3
  201.8 1.8 convert_element_type.72
  203.7 0.0 copy-done.3
  203.7 2.6 fusion.14
  206.3 0.0 all-gather.3.cloned.1.call-update
  206.3 0.0 all-gather.5.cloned.1.call-start
  206.4 0.5 all-gather.5.cloned.1.call-update
  206.9 13.5 %convolution_convert_fusion.4 = bf16[8,64,1024]{2,1,0:T(8,128)(2,1)S(1)} fusion(bf16[8,1536,1024]{2,1,0:T(8,128)(2,1)} %param.13, bf16[8,64,1536]{2,1,0:T(8,128)(2,1)S(1)} %copy-done.2, bf16[8,64,1536]{2,1,0:T(8,128)(2,1)} %get-tuple-element.6), kind=kOutput, calls=%fused_computation.7 | convolution fusion | flops 1617428480 | bytes 29360128 | tf_op jit(solution)/shard_map/erf,efd->erd/dot_general | solution.py:48
  220.4 1.6 copy.51
  222.0 4.6 %all-to-all-start.1 = ((bf16[8,64,1024]{2,0,1:T(8,128)(2,1)}), bf16[8,64,1024]{2,0,1:T(8,128)(2,1)}, u32[]{:S(2)}, u32[]{:S(2)}) async-start(bf16[8,64,1024]{2,0,1:T(8,128)(2,1)} %copy.51), calls=%async_computation.1 | async-start | bytes 2097152 | tf_op jit(solution)/shard_map/all_to_all | solution.py:72
  226.6 10.6 %all-gather.3.cloned.1.call-done = bf16[8,64,1536]{2,1,0:T(8,128)(2,1)} async-done(((bf16[8,64,384]{2,1,0:T(8,128)(2,1)}), bf16[8,64,1536]{2,1,0:T(8,128)(2,1)}) %all-gather.3.cloned.1.call-update) | async-done | bytes 1572880 | tf_op jit(solution)/shard_map/all_gather | solution.py:64
  237.2 13.8 %fusion.21 = f32[8,64,1024]{2,1,0:T(8,128)} fusion(bf16[8,64,1536]{2,1,0:T(8,128)(2,1)} %all-gather.3.cloned.1.call-done, bf16[8,1024,1536]{2,1,0:T(8,128)(2,1)} %param.11), kind=kOutput, calls=%fused_computation.44 | convolution fusion | flops 1610612736 | bytes 28835840 | tf_op jit(solution)/shard_map/erf,edf->erd/dot_general | solution.py:66
  251.0 18.6 %all-gather.5.cloned.1.call-done = bf16[8,64,1536]{2,1,0:T(8,128)(2,1)} async-done(((bf16[8,64,384]{2,1,0:T(8,128)(2,1)}), bf16[8,64,1536]{2,1,0:T(8,128)(2,1)}) %all-gather.5.cloned.1.call-update) | async-done | bytes 1572880 | tf_op jit(solution)/shard_map/all_gather | solution.py:65
  269.6 14.0 %add_convert_fusion = bf16[8,64,1024]{2,1,0:T(8,128)(2,1)} fusion(f32[8,64,1024]{2,1,0:T(8,128)} %fusion.21, bf16[8,64,1536]{2,1,0:T(8,128)(2,1)} %all-gather.5.cloned.1.call-done, bf16[8,1024,1536]{2,1,0:T(8,128)(2,1)} %param.12), kind=kOutput, calls=%fused_computation.6 | convolution fusion | flops 1611661312 | bytes 29884416 | tf_op jit(solution)/shard_map/erf,edf->erd/dot_general | solution.py:67
  283.6 2.8 copy.55
  286.3 0.0 all-to-all-done.1
  286.3 4.6 %all-to-all-start.3 = ((bf16[8,64,1024]{2,0,1:T(8,128)(2,1)}), bf16[8,64,1024]{2,0,1:T(8,128)(2,1)}, u32[]{:S(2)}, u32[]{:S(2)}) async-start(bf16[8,64,1024]{2,0,1:T(8,128)(2,1)} %copy.55), calls=%async_computation.3 | async-start | bytes 2097152 | tf_op jit(solution)/shard_map/all_to_all | solution.py:73
  291.0 13.8 %convolution_convert_fusion = bf16[8,1536,1024]{2,1,0:T(8,128)(2,1)} fusion(bf16[8,8,8,1024]{3,2,1,0:T(8,128)(2,1)S(1)} %bitcast.66, bf16[8,64,1536]{2,1,0:T(8,128)(2,1)S(1)} %copy-done.2, bf16[8,64,1536]{2,1,0:T(8,128)(2,1)} %get-tuple-element.6), kind=kOutput, calls=%fused_computation | convolution fusion | flops 1629487104 | bytes 29360128 | tf_op jit(solution)/shard_map/erf,erd->efd/dot_general | solution.py:51
  304.8 1.9 copy.53
  306.6 1.2 convolution_convert_fusion.8
  307.9 9.8 %all-to-all-done.3 = bf16[8,64,1024]{2,0,1:T(8,128)(2,1)} async-done(((bf16[8,64,1024]{2,0,1:T(8,128)(2,1)}), bf16[8,64,1024]{2,0,1:T(8,128)(2,1)}, u32[]{:S(2)}, u32[]{:S(2)}) %all-to-all-start.3) | async-done | bytes 1048608 | tf_op jit(solution)/shard_map/all_to_all | solution.py:73
  317.6 1.8 copy.57
  319.4 0.0 copy-done.5
  319.5 0.9 convolution_convert_fusion.7
  320.4 0.0 copy-done.1
  (6 shorter events, 0.1 us)
Async XLA Ops:
  7.2 3.9 %copy-start = (bf16[32,1024]{1,0:T(8,128)(2,1)S(1)}, bf16[32,1024]{1,0:T(8,128)(2,1)}, u32[]{:S(2)}) copy-start(bf16[32,1024]{1,0:T(8,128)(2,1)} %param.7) | copy-start | bytes 196612
  7.2 11.6 %copy-start.6 = (bf16[32,1024]{1,0:T(8,128)(2,1)S(1)}, bf16[32,1024]{1,0:T(8,128)(2,1)}, u32[]{:S(2)}) copy-start(bf16[32,1024]{1,0:T(8,128)(2,1)} %param.8) | copy-start | bytes 196612
  10.4 0.6 copy-start.4
  12.4 32.9 %all-to-all-start = ((bf16[64,8,1024]{2,1,0:T(8,128)(2,1)}), bf16[64,8,1024]{2,1,0:T(8,128)(2,1)S(1)}, u32[]{:S(2)}, u32[]{:S(2)}) async-start(bf16[64,8,1024]{2,1,0:T(8,128)(2,1)} %fusion), calls=%async_computation | async-start | bytes 2097152 | tf_op jit(solution)/shard_map/all_to_all | solution.py:36
  45.4 31.1 %all-to-all-start.2 = ((bf16[64,8,1024]{2,1,0:T(8,128)(2,1)}), bf16[64,8,1024]{2,1,0:T(8,128)(2,1)S(1)}, u32[]{:S(2)}, u32[]{:S(2)}) async-start(bf16[64,8,1024]{2,1,0:T(8,128)(2,1)} %fusion.1), calls=%async_computation.2 | async-start | bytes 2097152 | tf_op jit(solution)/shard_map/all_to_all | solution.py:37
  48.9 116.0 %all-reduce.3.cloned.1.call-start = ((), (), s32[]{:S(2)}) async-start(), calls=%async_computation.8 | async-start | bytes 6291456 | tf_op jit(solution)/shard_map/psum | solution.py:43
  76.4 122.6 %reduce-scatter.4.cloned.1.call-start = ((), (), s32[]{:S(2)}) async-start(), calls=%async_computation.7 | async-start | bytes 1966080
  98.6 138.5 %all-gather.3.cloned.1.call-start = ((), (), s32[]{:S(2)}) async-start(), calls=%async_computation.5 | async-start | bytes 1966080 | tf_op jit(solution)/shard_map/all_gather | solution.py:64
  164.9 3.6 %copy-start.2 = (bf16[8,64,1536]{2,1,0:T(8,128)(2,1)S(1)}, bf16[8,64,1536]{2,1,0:T(8,128)(2,1)}, u32[]{:S(2)}) copy-start(bf16[8,64,1536]{2,1,0:T(8,128)(2,1)} %get-tuple-element.5) | copy-start | bytes 4718596
  201.8 1.9 copy-start.3
  206.3 63.3 %all-gather.5.cloned.1.call-start = ((), (), s32[]{:S(2)}) async-start(), calls=%async_computation.6 | async-start | bytes 1966080 | tf_op jit(solution)/shard_map/all_gather | solution.py:65
  222.0 64.3 %all-to-all-start.1 = ((bf16[8,64,1024]{2,0,1:T(8,128)(2,1)}), bf16[8,64,1024]{2,0,1:T(8,128)(2,1)}, u32[]{:S(2)}, u32[]{:S(2)}) async-start(bf16[8,64,1024]{2,0,1:T(8,128)(2,1)} %copy.51), calls=%async_computation.1 | async-start | bytes 2097152 | tf_op jit(solution)/shard_map/all_to_all | solution.py:72
  286.3 31.3 %all-to-all-start.3 = ((bf16[8,64,1024]{2,0,1:T(8,128)(2,1)}), bf16[8,64,1024]{2,0,1:T(8,128)(2,1)}, u32[]{:S(2)}, u32[]{:S(2)}) async-start(bf16[8,64,1024]{2,0,1:T(8,128)(2,1)} %copy.55), calls=%async_computation.3 | async-start | bytes 2097152 | tf_op jit(solution)/shard_map/all_to_all | solution.py:73
  304.8 14.7 %copy-start.5 = (bf16[32,512]{1,0:T(8,128)(2,1)S(1)}, bf16[32,512]{1,0:T(8,128)(2,1)}, u32[]{:S(2)}) copy-start(bf16[32,512]{1,0:T(8,128)(2,1)} %copy-done.4) | copy-start | bytes 98308
  304.8 15.6 %copy-start.1 = (bf16[32,1024]{1,0:T(8,128)(2,1)S(1)}, bf16[32,1024]{1,0:T(8,128)(2,1)}, u32[]{:S(2)}) copy-start(bf16[32,1024]{1,0:T(8,128)(2,1)} %param.7) | copy-start | bytes 196612
Sparse Core Ops, SparseCore 0:
  76.5 88.3 all-reduce.2
  167.9 31.1 reduce-scatter.3
  206.4 30.6 all-gather.2
  238.8 30.6 all-gather.4
where the time goes:
time: 328 us; the launch traced here: 327 us
  waiting for transfers between devices  158 us (48%)
  matrix products  101 us (31%)
  local copies, waits for them, and re-layouts  22.4 us (7%)
  starting transfers between devices  19.4 us (6%)
  between operations  13.9 us (4%)
  other arithmetic  11.7 us (4%)
    psum x1, waiting for transfers between devices, local(): lax.psum(pre_gate.astype(jnp.bfloat16), 'tensor').astype(jnp.float32)  66 us
    unnamed x5, waiting for transfers between devices  28.6 us
    all_to_all x1, waiting for transfers between devices, local(): lax.all_to_all(token_send, 'expert', split_axis=0, concat_axis=1, tiled=T...  24.5 us
    all_gather x1, waiting for transfers between devices, local(): up_piece = lax.all_gather(up_grad, 'tensor', axis=2, tiled=True)  18.6 us
    dot_general x1, matrix products, local(): jnp.einsum('erf,edf->erd', up_piece, w_up, preferred_element_type=jnp.flo...  14 us
    unnamed x20, local copies, waits for them, and re-layouts  13.9 us
    dot_general x1, matrix products, local(): jnp.einsum('erf,erd->efd', hidden, grad_rows, preferred_element_type=jnp....  13.8 us
    dot_general x1, matrix products, local(): jnp.einsum('erf,edf->erd', gate_piece, w_gate, preferred_element_type=jnp...  13.8 us
  transfers between devices with their start and end apart: 8, of which 6 were waited for; matrix products, arithmetic and copies ran while one was open for 37% of the time, Pallas kernels for 0%

commit v1 on v0

--- a/solution.py
+++ b/solution.py
@@ -2,6 +2,13 @@
 import jax.numpy as jnp
 from jax import lax
 from jax.sharding import PartitionSpec as P
+
+
+def exchange_blocks(x, name, split, join):
+    peers = lax.axis_size(name)
+    pieces = jnp.stack(jnp.split(x, peers, axis=split), axis=0)
+    pieces = lax.all_to_all(pieces, name, split_axis=0, concat_axis=0)
+    return jnp.concatenate(pieces, axis=join)
 
 
 def local(tokens, cotangent, expert_ids, route_weight, w_gate, w_up, w_down):
@@ -33,7 +40,7 @@
         experts, capacity, model_width
     )
     token_rows, grad_rows = (
-        lax.all_to_all(token_send, "expert", split_axis=0, concat_axis=1, tiled=True),
+        exchange_blocks(token_send, "expert", 0, 1),
         lax.all_to_all(gradient_outgoing, "expert", split_axis=0, concat_axis=1, tiled=True),
     )
     pre_gate = jnp.einsum("erd,edf->erf", token_rows, w_gate, preferred_element_type=jnp.float32)

time: 328 us -> 332 us (1.012)
  local copies, waits for them, and re-layouts: 22.4 us -> 27.7 us
    unnamed x20 -> x27, local copies, waits for them, and re-layouts: 13.9 us -> 18.5 us
  transfers between devices with their start and end apart: 8 -> 8, of which waited for: 6 -> 6; matrix products, arithmetic and copies ran while one was open for 37% -> 36% of each run, Pallas kernels for 0% -> 0%
where the time goes in v1:
time: 332 us; the launch traced here: 331 us
  waiting for transfers between devices  158 us (48%)
  matrix products  100 us (30%)
  local copies, waits for them, and re-layouts  27.7 us (8%)
  starting transfers between devices  19.4 us (6%)
  between operations  13.9 us (4%)
  other arithmetic  11.7 us (4%)
    psum x1, waiting for transfers between devices, local(): lax.psum(pre_gate.astype(jnp.bfloat16), 'tensor').astype(jnp.float32)  66 us
    unnamed x5, waiting for transfers between devices  28.6 us
    all_to_all x1, waiting for transfers between devices, exchange_blocks(): pieces = lax.all_to_all(pieces, name, split_axis=0, concat_axis=0)  24.5 us
    all_gather x1, waiting for transfers between devices, local(): up_piece = lax.all_gather(up_grad, 'tensor', axis=2, tiled=True)  18.6 us
    unnamed x27, local copies, waits for them, and re-layouts  18.5 us
    dot_general x1, matrix products, local(): jnp.einsum('erf,edf->erd', up_piece, w_up, preferred_element_type=jnp.flo...  14 us
    dot_general x1, matrix products, local(): jnp.einsum('erf,erd->efd', hidden, grad_rows, preferred_element_type=jnp....  13.8 us
    dot_general x1, matrix products, local(): jnp.einsum('erf,edf->erd', gate_piece, w_gate, preferred_element_type=jnp...  13.8 us
  transfers between devices with their start and end apart: 8, of which 6 were waited for; matrix products, arithmetic and copies ran while one was open for 36% of the time, Pallas kernels for 0%

profile of v1, /device:TPU:0, one launch (start us, length us, event | category | flops | bytes accessed | tf_op | source)
XLA Modules:
  0.0 331.3 jit_solution(13904371478443951147)
XLA Ops:
  7.2 0.0 copy-start
  7.2 0.8 copy.45
  8.0 0.1 eq.43
  8.1 0.1 eq.39
  8.2 0.8 copy.49
  8.9 0.6 reduce-window.6
  9.6 0.2 slice_reduce_fusion
  9.8 0.1 fusion.24
  9.9 0.1 reduce_sum.30
  10.0 0.4 convert_reduce_fusion
  10.4 0.0 copy-start.4
  10.4 0.6 copy-done.4
  11.0 0.5 convolution_convert_fusion.6
  11.5 0.7 fusion.21
  12.1 0.7 fusion.20
  12.8 0.7 fusion.19
  13.5 0.7 fusion.18
  14.1 0.7 fusion.17
  14.8 0.7 fusion.16
  15.5 0.7 fusion.15
  16.1 0.7 fusion.14
  16.8 6.3 %all-to-all-start = ((bf16[8,8,8,1024]{3,2,1,0:T(8,128)(2,1)}), bf16[8,8,8,1024]{3,2,1,0:T(8,128)(2,1)S(1)}, u32[]{:S(2)}, u32[]{:S(2)}) async-start(bf16[8,8,8,1024]{3,2,1,0:T(8,128)(2,1)} %fusion.14), calls=%async_computation | async-start | bytes 2097152 | tf_op jit(solution)/shard_map/all_to_all | solution.py:10
  23.2 2.0 fusion
  25.2 24.5 %all-to-all-done = bf16[8,8,8,1024]{3,2,1,0:T(8,128)(2,1)S(1)} async-done(((bf16[8,8,8,1024]{3,2,1,0:T(8,128)(2,1)}), bf16[8,8,8,1024]{3,2,1,0:T(8,128)(2,1)S(1)}, u32[]{:S(2)}, u32[]{:S(2)}) %all-to-all-start) | async-done | bytes 1048608 | tf_op jit(solution)/shard_map/all_to_all | solution.py:10
  49.7 3.6 %all-to-all-start.2 = ((bf16[64,8,1024]{2,1,0:T(8,128)(2,1)}), bf16[64,8,1024]{2,1,0:T(8,128)(2,1)S(1)}, u32[]{:S(2)}, u32[]{:S(2)}) async-start(bf16[64,8,1024]{2,1,0:T(8,128)(2,1)} %fusion), calls=%async_computation.2 | async-start | bytes 2097152 | tf_op jit(solution)/shard_map/all_to_all | solution.py:44
  53.3 0.0 all-reduce.3.cloned.1.call-start
  53.3 13.7 %convolution_convert_fusion.2 = bf16[8,64,1536]{2,1,0:T(8,128)(2,1)} fusion(bf16[8,1024,1536]{2,1,0:T(8,128)(2,1)} %param.12, bf16[8,8,8,1024]{3,2,1,0:T(8,128)(2,1)S(1)} %all-to-all-done), kind=kOutput, calls=%fused_computation.4 | convolution fusion | flops 1611399168 | bytes 27787264 | tf_op jit(solution)/shard_map/erd,edf->erf/dot_general | solution.py:47
  67.0 13.7 %convolution_convert_fusion.3 = bf16[8,64,1536]{2,1,0:T(8,128)(2,1)} fusion(bf16[8,1024,1536]{2,1,0:T(8,128)(2,1)} %param.11, bf16[8,8,8,1024]{3,2,1,0:T(8,128)(2,1)S(1)} %all-to-all-done), kind=kOutput, calls=%fused_computation.5 | convolution fusion | flops 1611399168 | bytes 27787264 | tf_op jit(solution)/shard_map/erd,edf->erf/dot_general | solution.py:46
  80.7 0.0 all-reduce.3.cloned.1.call-update
  80.8 0.2 reduce-scatter.4.cloned.1.call-start
  81.0 0.0 all-to-all-done.2
  81.0 13.2 %convolution_convert_fusion.1 = bf16[8,64,1536]{2,1,0:T(8,128)(2,1)S(1)} fusion(bf16[8,1536,1024]{2,1,0:T(8,128)(2,1)} %param.13, bf16[8,8,8,1024]{3,2,1,0:T(8,128)(2,1)S(1)} %bitcast.99), kind=kOutput, calls=%fused_computation.3 | convolution fusion | flops 1611399168 | bytes 27787264 | tf_op jit(solution)/shard_map/erd,efd->erf/dot_general | solution.py:63
  94.2 3.5 %copy.60 = bf16[8,64,1536]{1,0,2:T(8,128)(2,1)} copy(bf16[8,64,1536]{2,1,0:T(8,128)(2,1)S(1)} %convolution_convert_fusion.1) | data formatting | bytes 3145728
  97.7 5.4 %reshape.82 = bf16[1536,512]{1,0:T(8,128)(2,1)} reshape(bf16[1536,8,64]{2,1,0:T(8,128)(2,1)} %bitcast.101) | data formatting | bytes 3145728
  103.1 0.0 reduce-scatter.4.cloned.1.call-update
  103.1 0.0 all-gather.3.cloned.1.call-start
  103.2 66.0 %all-reduce.3.cloned.1.call-done = (bf16[8,64,1536]{2,1,0:T(8,128)(2,1)}, bf16[8,64,1536]{2,1,0:T(8,128)(2,1)}) async-done(((bf16[8,64,1536]{2,1,0:T(8,128)(2,1)}, bf16[8,64,1536]{2,1,0:T(8,128)(2,1)}), (bf16[8,64,1536]{2,1,0:T(8,128)(2,1)}, bf16[8,64,1536]{2,1,0:T(8,128)(2,1)})) %all-reduce.3.cloned.1.call-update) | async-done | bytes 3145744 | tf_op jit(solution)/shard_map/psum | solution.py:50
  169.2 3.6 %convert_element_type.70 = f32[8,64,1536]{2,1,0:T(8,128)} convert(bf16[8,64,1536]{2,1,0:T(8,128)(2,1)} %get-tuple-element.5) | non-fusion elementwise | flops 786432 | bytes 4718592 | tf_op jit(solution)/shard_map/convert_element_type | solution.py:50
  172.8 0.0 copy-done.2
  172.8 2.5 add_divide_fusion
  175.3 28.1 %reduce-scatter.4.cloned.1.call-done = bf16[384,512]{1,0:T(8,128)(2,1)} async-done(((bf16[1536,512]{1,0:T(8,128)(2,1)}), bf16[384,512]{1,0:T(8,128)(2,1)}) %reduce-scatter.4.cloned.1.call-update) | async-done | bytes 393232
  203.4 1.5 reshape.83
  204.9 1.3 copy.61
  206.2 1.8 convert_element_type.72
  208.1 2.6 fusion.13
  210.6 0.0 all-gather.3.cloned.1.call-update
  210.7 0.0 all-gather.5.cloned.1.call-start
  210.7 0.5 all-gather.5.cloned.1.call-update
  211.2 13.5 %convolution_convert_fusion.4 = bf16[8,64,1024]{2,1,0:T(8,128)(2,1)S(1)} fusion(bf16[8,1536,1024]{2,1,0:T(8,128)(2,1)} %param.13, bf16[8,64,1536]{2,1,0:T(8,128)(2,1)S(1)} %copy-done.2, bf16[8,64,1536]{2,1,0:T(8,128)(2,1)} %get-tuple-element.6), kind=kOutput, calls=%fused_computation.7 | convolution fusion | flops 1617428480 | bytes 29360128 | tf_op jit(solution)/shard_map/erf,efd->erd/dot_general | solution.py:55
  224.8 1.6 copy.51
  226.4 4.6 %all-to-all-start.1 = ((bf16[8,64,1024]{2,0,1:T(8,128)(2,1)}), bf16[8,64,1024]{2,0,1:T(8,128)(2,1)}, u32[]{:S(2)}, u32[]{:S(2)}) async-start(bf16[8,64,1024]{2,0,1:T(8,128)(2,1)} %copy.51), calls=%async_computation.1 | async-start | bytes 2097152 | tf_op jit(solution)/shard_map/all_to_all | solution.py:79
  230.9 10.6 %all-gather.3.cloned.1.call-done = bf16[8,64,1536]{2,1,0:T(8,128)(2,1)} async-done(((bf16[8,64,384]{2,1,0:T(8,128)(2,1)}), bf16[8,64,1536]{2,1,0:T(8,128)(2,1)}) %all-gather.3.cloned.1.call-update) | async-done | bytes 1572880 | tf_op jit(solution)/shard_map/all_gather | solution.py:71
  241.5 13.8 %fusion.28 = f32[8,64,1024]{2,1,0:T(8,128)} fusion(bf16[8,64,1536]{2,1,0:T(8,128)(2,1)} %all-gather.3.cloned.1.call-done, bf16[8,1024,1536]{2,1,0:T(8,128)(2,1)} %param.11), kind=kOutput, calls=%fused_computation.59 | convolution fusion | flops 1610612736 | bytes 28835840 | tf_op jit(solution)/shard_map/erf,edf->erd/dot_general | solution.py:73
  255.3 18.6 %all-gather.5.cloned.1.call-done = bf16[8,64,1536]{2,1,0:T(8,128)(2,1)} async-done(((bf16[8,64,384]{2,1,0:T(8,128)(2,1)}), bf16[8,64,1536]{2,1,0:T(8,128)(2,1)}) %all-gather.5.cloned.1.call-update) | async-done | bytes 1572880 | tf_op jit(solution)/shard_map/all_gather | solution.py:72
  273.9 14.0 %add_convert_fusion = bf16[8,64,1024]{2,1,0:T(8,128)(2,1)} fusion(f32[8,64,1024]{2,1,0:T(8,128)} %fusion.28, bf16[8,64,1536]{2,1,0:T(8,128)(2,1)} %all-gather.5.cloned.1.call-done, bf16[8,1024,1536]{2,1,0:T(8,128)(2,1)} %param.12), kind=kOutput, calls=%fused_computation.6 | convolution fusion | flops 1611661312 | bytes 29884416 | tf_op jit(solution)/shard_map/erf,edf->erd/dot_general | solution.py:74
  287.9 2.8 copy.55
  290.7 0.0 all-to-all-done.1
  290.7 4.6 %all-to-all-start.3 = ((bf16[8,64,1024]{2,0,1:T(8,128)(2,1)}), bf16[8,64,1024]{2,0,1:T(8,128)(2,1)}, u32[]{:S(2)}, u32[]{:S(2)}) async-start(bf16[8,64,1024]{2,0,1:T(8,128)(2,1)} %copy.55), calls=%async_computation.3 | async-start | bytes 2097152 | tf_op jit(solution)/shard_map/all_to_all | solution.py:80
  295.3 13.8 %convolution_convert_fusion = bf16[8,1536,1024]{2,1,0:T(8,128)(2,1)} fusion(bf16[8,8,8,1024]{3,2,1,0:T(8,128)(2,1)S(1)} %bitcast.100, bf16[8,64,1536]{2,1,0:T(8,128)(2,1)S(1)} %copy-done.2, bf16[8,64,1536]{2,1,0:T(8,128)(2,1)} %get-tuple-element.6), kind=kOutput, calls=%fused_computation | convolution fusion | flops 1629487104 | bytes 29360128 | tf_op jit(solution)/shard_map/erf,erd->efd/dot_general | solution.py:58
  309.1 1.9 copy.53
  311.0 1.2 convolution_convert_fusion.8
  312.2 9.8 %all-to-all-done.3 = bf16[8,64,1024]{2,0,1:T(8,128)(2,1)} async-done(((bf16[8,64,1024]{2,0,1:T(8,128)(2,1)}), bf16[8,64,1024]{2,0,1:T(8,128)(2,1)}, u32[]{:S(2)}, u32[]{:S(2)}) %all-to-all-start.3) | async-done | bytes 1048608 | tf_op jit(solution)/shard_map/all_to_all | solution.py:80
  322.0 1.8 copy.57
  323.8 0.9 convolution_convert_fusion.7
  (14 shorter events, 0.1 us)
Async XLA Ops:
  7.2 3.9 %copy-start = (bf16[32,1024]{1,0:T(8,128)(2,1)S(1)}, bf16[32,1024]{1,0:T(8,128)(2,1)}, u32[]{:S(2)}) copy-start(bf16[32,1024]{1,0:T(8,128)(2,1)} %param.7) | copy-start | bytes 196612
  7.2 16.0 %copy-start.6 = (bf16[32,1024]{1,0:T(8,128)(2,1)S(1)}, bf16[32,1024]{1,0:T(8,128)(2,1)}, u32[]{:S(2)}) copy-start(bf16[32,1024]{1,0:T(8,128)(2,1)} %param.8) | copy-start | bytes 196612
  10.4 0.6 copy-start.4
  16.8 32.9 %all-to-all-start = ((bf16[8,8,8,1024]{3,2,1,0:T(8,128)(2,1)}), bf16[8,8,8,1024]{3,2,1,0:T(8,128)(2,1)S(1)}, u32[]{:S(2)}, u32[]{:S(2)}) async-start(bf16[8,8,8,1024]{3,2,1,0:T(8,128)(2,1)} %fusion.14), calls=%async_computation | async-start | bytes 2097152 | tf_op jit(solution)/shard_map/all_to_all | solution.py:10
  49.7 31.3 %all-to-all-start.2 = ((bf16[64,8,1024]{2,1,0:T(8,128)(2,1)}), bf16[64,8,1024]{2,1,0:T(8,128)(2,1)S(1)}, u32[]{:S(2)}, u32[]{:S(2)}) async-start(bf16[64,8,1024]{2,1,0:T(8,128)(2,1)} %fusion), calls=%async_computation.2 | async-start | bytes 2097152 | tf_op jit(solution)/shard_map/all_to_all | solution.py:44
  53.3 116.0 %all-reduce.3.cloned.1.call-start = ((), (), s32[]{:S(2)}) async-start(), calls=%async_computation.8 | async-start | bytes 6291456 | tf_op jit(solution)/shard_map/psum | solution.py:50
  80.8 122.6 %reduce-scatter.4.cloned.1.call-start = ((), (), s32[]{:S(2)}) async-start(), calls=%async_computation.7 | async-start | bytes 1966080
  103.1 138.4 %all-gather.3.cloned.1.call-start = ((), (), s32[]{:S(2)}) async-start(), calls=%async_computation.5 | async-start | bytes 1966080 | tf_op jit(solution)/shard_map/all_gather | solution.py:71
  169.2 3.6 %copy-start.2 = (bf16[8,64,1536]{2,1,0:T(8,128)(2,1)S(1)}, bf16[8,64,1536]{2,1,0:T(8,128)(2,1)}, u32[]{:S(2)}) copy-start(bf16[8,64,1536]{2,1,0:T(8,128)(2,1)} %get-tuple-element.5) | copy-start | bytes 4718596
  206.2 1.9 copy-start.3
  210.7 63.3 %all-gather.5.cloned.1.call-start = ((), (), s32[]{:S(2)}) async-start(), calls=%async_computation.6 | async-start | bytes 1966080 | tf_op jit(solution)/shard_map/all_gather | solution.py:72
  226.4 64.3 %all-to-all-start.1 = ((bf16[8,64,1024]{2,0,1:T(8,128)(2,1)}), bf16[8,64,1024]{2,0,1:T(8,128)(2,1)}, u32[]{:S(2)}, u32[]{:S(2)}) async-start(bf16[8,64,1024]{2,0,1:T(8,128)(2,1)} %copy.51), calls=%async_computation.1 | async-start | bytes 2097152 | tf_op jit(solution)/shard_map/all_to_all | solution.py:79
  290.7 31.3 %all-to-all-start.3 = ((bf16[8,64,1024]{2,0,1:T(8,128)(2,1)}), bf16[8,64,1024]{2,0,1:T(8,128)(2,1)}, u32[]{:S(2)}, u32[]{:S(2)}) async-start(bf16[8,64,1024]{2,0,1:T(8,128)(2,1)} %copy.55), calls=%async_computation.3 | async-start | bytes 2097152 | tf_op jit(solution)/shard_map/all_to_all | solution.py:80
  309.1 14.7 %copy-start.5 = (bf16[32,512]{1,0:T(8,128)(2,1)S(1)}, bf16[32,512]{1,0:T(8,128)(2,1)}, u32[]{:S(2)}) copy-start(bf16[32,512]{1,0:T(8,128)(2,1)} %copy-done.4) | copy-start | bytes 98308
  309.1 15.6 %copy-start.1 = (bf16[32,1024]{1,0:T(8,128)(2,1)S(1)}, bf16[32,1024]{1,0:T(8,128)(2,1)}, u32[]{:S(2)}) copy-start(bf16[32,1024]{1,0:T(8,128)(2,1)} %param.7) | copy-start | bytes 196612
Sparse Core Ops, SparseCore 0:
  80.9 88.3 all-reduce.2
  172.2 31.1 reduce-scatter.3
  210.8 30.6 all-gather.2
  243.2 30.6 all-gather.4
